TPU v7x, 128 devices: a whole 4x4x4 slice. The times are simulated.
128 devices in a mesh: dp: 8 (over y, core), expert: 16 (over z, x).
Axes of the slice: x: 4, y: 4, z: 4, core: 2. Of those that a mesh axis runs over, the one named last changes fastest.
Arguments:
- tokens: bfloat16 [32768, 2048], P(('dp', 'expert')), parts along dimension 0, may hold values from -6 to 6
- target: int32 [32768, 8], P(('dp', 'expert')), parts along dimension 0, may hold values from 0 to 47, as said below
- router_weight: float32 [32768, 8], P(('dp', 'expert')), parts along dimension 0, may hold values from 0.1 to 1
- replica_pick: int32 [128], P(('dp', 'expert')), parts along dimension 0, may hold values from 0 to 1
- w_gate: bfloat16 [32, 2048, 768], P('expert'), may hold values from -0.125 to 0.125
- w_up: bfloat16 [32, 2048, 768], P('expert'), may hold values from -0.125 to 0.125
- w_down: bfloat16 [32, 768, 2048], P('expert'), may hold values from -0.21875 to 0.21875
Outputs:
- mixed: bfloat16 [32768, 2048], P(('dp', 'expert')), parts along dimension 0
There are 8 independent parts, one for each index of `dp`. A program takes and returns all parts, laid end to end along the dimension named above; an argument that names none is the same for every part. Nothing has to cross between parts.
Inputs may be any that keep to these rules, and one draw needn't show every extreme that they name: `target`: within each aligned block of 256 rows (one device's tokens) no slot is named more than 64 times, and at least one slot, the same one in every block, is named exactly 64 times in every block (other slots may also reach 64); the 8 slots of a row name 8 different experts.
All inputs are finite; a program needn't handle non-finite values.
Results may differ from a plain program's by a relative error of at most 0.008.
Values may be sent and summed in bfloat16 or wider, within the bound.
A program may use at most 192 MiB of HBM per device.

v0:
```python
import jax
import jax.numpy as jnp
from jax import lax
from jax.sharding import PartitionSpec as P


def shifted(value, axis, steps):
    count = lax.axis_size(axis)
    pairs = [(source, (source + steps) % count) for source in range(count)]
    return lax.ppermute(value, axis, pairs)


def body(tokens, target, router_weight, replica_pick, w_gate, w_up, w_down):
    tok_rows, width = tokens.shape
    top = target.shape[1]
    per_device = w_gate.shape[0]
    slots = per_device + 1
    groups = lax.axis_size("expert")
    virtual = groups * slots
    capacity = 3 * tok_rows * top // (2 * virtual)
    flat = target.reshape(-1)
    onehot = (flat[:, None] == jnp.arange(virtual, dtype=jnp.int32)[None, :]).astype(jnp.int32)
    earlier = jnp.cumsum(onehot, axis=0) - onehot
    place = jnp.sum(earlier * onehot, axis=1)
    row_index = flat * capacity + place
    buffer = jnp.zeros((virtual * capacity, width), jnp.bfloat16)
    buffer = buffer.at[row_index].set(jnp.repeat(tokens, top, axis=0), unique_indices=True)
    outgoing = buffer.reshape(groups, slots, capacity, width)
    lent = replica_pick[0]
    own_gate = lax.dynamic_index_in_dim(w_gate, lent, 0, keepdims=False)
    own_up = lax.dynamic_index_in_dim(w_up, lent, 0, keepdims=False)
    own_down = lax.dynamic_index_in_dim(w_down, lent, 0, keepdims=False)
    spare_gate, spare_up, spare_down = shifted((own_gate, own_up, own_down), "expert", 1)
    rows = lax.all_to_all(outgoing, "expert", split_axis=0, concat_axis=0, tiled=True)
    owned = rows[:, :per_device]
    gate = jnp.einsum("nscd,sdf->nscf", owned, w_gate, preferred_element_type=jnp.float32)
    upper = jnp.einsum("nscd,sdf->nscf", owned, w_up, preferred_element_type=jnp.float32)
    hidden = (jax.nn.silu(gate) * upper).astype(jnp.bfloat16)
    result = jnp.einsum(
        "nscf,sfd->nscd", hidden, w_down, preferred_element_type=jnp.float32
    ).astype(jnp.bfloat16)
    spare_rows = rows[:, per_device]
    gate_two = jnp.einsum("ncd,df->ncf", spare_rows, spare_gate, preferred_element_type=jnp.float32)
    upper_two = jnp.einsum("ncd,df->ncf", spare_rows, spare_up, preferred_element_type=jnp.float32)
    hidden_two = (jax.nn.silu(gate_two) * upper_two).astype(jnp.bfloat16)
    result_two = jnp.einsum(
        "ncf,fd->ncd", hidden_two, spare_down, preferred_element_type=jnp.float32
    ).astype(jnp.bfloat16)
    results = jnp.concatenate([result, result_two[:, None]], axis=1)
    returned = lax.all_to_all(results, "expert", split_axis=0, concat_axis=0, tiled=True)
    picked = returned.reshape(virtual * capacity, width)[row_index].reshape(tok_rows, top, width)
    share = router_weight / jnp.sum(router_weight, axis=1, keepdims=True)
    mixed = jnp.sum(share[:, :, None] * picked.astype(jnp.float32), axis=1)
    return mixed.astype(jnp.bfloat16)


def solution(mesh):
    in_specs = (
        P(("dp", "expert"), None),
        P(("dp", "expert"), None),
        P(("dp", "expert"), None),
        P(("dp", "expert")),
        P("expert", None, None),
        P("expert", None, None),
        P("expert", None, None),
    )
    out_specs = P(("dp", "expert"), None)
    return jax.shard_map(body, mesh=mesh, in_specs=in_specs, out_specs=out_specs, check_vma=False)
```

profile of v0, /device:TPU:0, one launch (start us, length us, event | category | flops | bytes accessed | tf_op | source)
XLA Modules:
  0.0 678.1 jit_solution(16677174123277555924)
XLA Ops:
  0.0 0.0 copy-start
  0.0 0.9 copy.19
  0.9 0.1 eq.29
  1.0 0.1 eq.25
  1.1 0.7 broadcast_multiply_fusion
  1.9 13.6 %reduce-window.6 = s32[48,16,128]{2,1,0:T(8,128)S(1)} reduce-window(s32[48,16,128]{2,1,0:T(8,128)S(1)} %fusion.34, s32[]{:T(128)} %constant.27.clone.1), window={size=1x1x128 pad=0_0x0_0x127_0}, to_apply=%region_1.2 | reduce-window | flops 12484608 | bytes 786436 | tf_op jit(solution)/shard_map/reduce-window
  15.5 0.2 slice.18
  15.7 0.3 copy.29
  16.0 0.2 reduce-window.9
  16.2 0.2 broadcast_add_fusion
  16.4 0.1 copy.18
  16.5 0.1 mul.44
  16.6 0.2 fusion.33
  16.8 0.0 copy-done
  16.8 19.1 %scatter_custom_fusion = bf16[3072,2048]{1,0:T(8,128)(2,1)} fusion(s32[2048]{0:T(1024)S(1)} %bitcast.114, bf16[]{:T(256)} %constant.18.clone.1, bf16[256,2048]{1,0:T(8,128)(2,1)S(1)} %copy-done), kind=kCustom, calls=%fused_computation.5 | custom fusion | bytes 13631490 | tf_op jit(solution)/shard_map/scatter | solution.py:27
  36.0 8.0 %all-to-all-start = ((bf16[16,3,64,2048]{3,2,1,0:T(8,128)(2,1)}), bf16[16,3,64,2048]{3,2,1,0:T(8,128)(2,1)}, u32[]{:S(2)}, u32[]{:S(2)}) async-start(bf16[16,3,64,2048]{3,2,1,0:T(8,128)(2,1)} %bitcast.107), calls=%async_computation | async-start | bytes 25165824 | tf_op jit(solution)/shard_map/all_to_all | solution.py:34
  44.7 0.0 slice-start
  44.7 0.0 slice-start.1
  44.7 4.0 dynamic-slice_bitcast_fusion.1
  48.7 1.9 collective-permute-start.1
  50.6 3.8 dynamic-slice_bitcast_fusion.2
  54.4 1.6 collective-permute-start
  56.0 0.0 slice-done
  56.0 0.0 slice-done.1
  56.0 1.9 dynamic-slice_bitcast_fusion
  57.8 1.2 collective-permute-start.2
  59.0 173.4 %all-to-all-done = bf16[16,3,64,2048]{3,2,1,0:T(8,128)(2,1)} async-done(((bf16[16,3,64,2048]{3,2,1,0:T(8,128)(2,1)}), bf16[16,3,64,2048]{3,2,1,0:T(8,128)(2,1)}, u32[]{:S(2)}, u32[]{:S(2)}) %all-to-all-start) | async-done | bytes 12582944 | tf_op jit(solution)/shard_map/all_to_all | solution.py:34
  232.5 12.6 %fusion.3 = f32[2,16,64,768]{3,2,1,0:T(8,128)} fusion(bf16[2,2048,768]{2,1,0:T(8,128)(2,1)} %param.12, bf16[16,3,64,2048]{3,2,1,0:T(8,128)(2,1)} %all-to-all-done), kind=kOutput, calls=%fused_computation.8 | convolution fusion | flops 6442450944 | bytes 20971520 | tf_op jit(solution)/shard_map/nscd,sdf->nscf/dot_general | solution.py:37
  245.0 34.9 %collective-permute-done.1 = bf16[2048,768]{1,0:T(8,128)(2,1)} collective-permute-done((bf16[2048,768]{1,0:T(8,128)(2,1)}, bf16[2048,768]{1,0:T(8,128)(2,1)}, u32[]{:S(2)}, u32[]{:S(2)}) %collective-permute-start.1) | collective-permute-done | bytes 3145760 | tf_op jit(solution)/shard_map/ppermute | solution.py:10
  279.9 8.3 %fusion.19 = f32[16,64,768]{2,1,0:T(8,128)} fusion(bf16[16,3,64,2048]{3,2,1,0:T(8,128)(2,1)} %all-to-all-done, bf16[2048,768]{1,0:T(8,128)(2,1)} %collective-permute-done.1), kind=kOutput, calls=%fused_computation.27 | convolution fusion | flops 3221225472 | bytes 10485760 | tf_op jit(solution)/shard_map/ncd,df->ncf/dot_general | solution.py:44
  288.2 22.2 %convert_bitcast_fusion = bf16[16,2,64,2048]{3,2,0,1:T(8,128)(2,1)} fusion(bf16[2,768,2048]{2,1,0:T(8,128)(2,1)} %param.13, f32[2,16,64,768]{3,2,1,0:T(8,128)} %fusion.3, bf16[2,2048,768]{2,1,0:T(8,128)(2,1)} %param.11, bf16[16,3,64,2048]{3,2,1,0:T(8,128)(2,1)} %all-to-all-done), kind=kOutput, calls=%fused_computation.7 | convolution fusion | flops 12898533376 | bytes 35651584 | tf_op jit(solution)/shard_map/nscf,sfd->nscd/dot_general | solution.py:39
  310.4 36.9 %collective-permute-done = bf16[2048,768]{1,0:T(8,128)(2,1)} collective-permute-done((bf16[2048,768]{1,0:T(8,128)(2,1)}, bf16[2048,768]{1,0:T(8,128)(2,1)}, u32[]{:S(2)}, u32[]{:S(2)}) %collective-permute-start) | collective-permute-done | bytes 3145760 | tf_op jit(solution)/shard_map/ppermute | solution.py:10
  347.3 66.3 %collective-permute-done.2 = bf16[768,2048]{1,0:T(8,128)(2,1)} collective-permute-done((bf16[768,2048]{1,0:T(8,128)(2,1)}, bf16[768,2048]{1,0:T(8,128)(2,1)}, u32[]{:S(2)}, u32[]{:S(2)}) %collective-permute-start.2) | collective-permute-done | bytes 3145760 | tf_op jit(solution)/shard_map/ppermute | solution.py:10
  413.6 13.5 %convert_bitcast_fusion.1 = bf16[16,1,64,2048]{3,2,0,1:T(8,128)(2,1)} fusion(bf16[768,2048]{1,0:T(8,128)(2,1)} %collective-permute-done.2, f32[16,64,768]{2,1,0:T(8,128)} %fusion.19, bf16[16,3,64,2048]{3,2,1,0:T(8,128)(2,1)} %all-to-all-done, bf16[2048,768]{1,0:T(8,128)(2,1)} %collective-permute-done), kind=kOutput, calls=%fused_computation.25 | convolution fusion | flops 6449266688 | bytes 17825792 | tf_op jit(solution)/shard_map/ncf,fd->ncd/dot_general | solution.py:46
  427.1 5.4 pad_maximum_fusion
  432.5 5.1 copy.25
  437.6 0.0 copy-start.2
  437.6 22.5 %all-to-all-start.1 = ((bf16[16,3,64,2048]{3,2,1,0:T(8,128)(2,1)}), bf16[16,3,64,2048]{3,2,1,0:T(8,128)(2,1)}, u32[]{:S(2)}, u32[]{:S(2)}) async-start(bf16[16,3,64,2048]{3,2,1,0:T(8,128)(2,1)} %copy.25), calls=%async_computation.1 | async-start | bytes 25165824 | tf_op jit(solution)/shard_map/all_to_all | solution.py:50
  460.1 0.0 copy-done.2
  460.2 0.1 copy.17
  460.3 182.5 %all-to-all-done.1 = bf16[16,3,64,2048]{3,2,1,0:T(8,128)(2,1)} async-done(((bf16[16,3,64,2048]{3,2,1,0:T(8,128)(2,1)}), bf16[16,3,64,2048]{3,2,1,0:T(8,128)(2,1)}, u32[]{:S(2)}, u32[]{:S(2)}) %all-to-all-start.1) | async-done | bytes 12582944 | tf_op jit(solution)/shard_map/all_to_all | solution.py:50
  642.8 0.0 copy-start.1
  642.8 22.6 %gather_fusion = bf16[2048,2048]{1,0:T(8,128)(2,1)} fusion(bf16[3072,2048]{1,0:T(8,128)(2,1)} %bitcast.25, s32[2048]{0:T(1024)S(1)} %broadcast_clamp_fusion), kind=kCustom, calls=%fused_computation | custom fusion | bytes 16785408 | tf_op jit(solution)/shard_map/gather | solution.py:51
  665.4 12.2 %fusion = bf16[256,2048]{1,0:T(8,128)(2,1)} fusion(bf16[2048,2048]{1,0:T(8,128)(2,1)} %gather_fusion, f32[256,8]{1,0:T(8,128)S(1)} %copy.17), kind=kLoop, calls=%fused_computation.3 | loop fusion | flops 12058624 | bytes 9445376 | tf_op jit(solution)/shard_map/reduce_sum | solution.py:53
  677.7 0.0 copy-done.1
  (6 shorter events, 0.1 us)
Async XLA Ops:
  0.0 16.8 %copy-start = (bf16[256,2048]{1,0:T(8,128)(2,1)S(1)}, bf16[256,2048]{1,0:T(8,128)(2,1)}, u32[]{:S(2)}) copy-start(bf16[256,2048]{1,0:T(8,128)(2,1)} %param.7) | copy-start | bytes 3145732
  36.0 196.5 %all-to-all-start = ((bf16[16,3,64,2048]{3,2,1,0:T(8,128)(2,1)}), bf16[16,3,64,2048]{3,2,1,0:T(8,128)(2,1)}, u32[]{:S(2)}, u32[]{:S(2)}) async-start(bf16[16,3,64,2048]{3,2,1,0:T(8,128)(2,1)} %bitcast.107), calls=%async_computation | async-start | bytes 25165824 | tf_op jit(solution)/shard_map/all_to_all | solution.py:34
  44.7 11.3 %slice-start = ((s8[6291456]{0:T(1024)(128)(4,1)}), s8[2097152]{0:T(1024)(128)(4,1)S(1)}, s32[]{:S(2)}) async-start(s8[6291456]{0:T(1024)(128)(4,1)} %bitcast.108), calls=%async_computation.2 | async-start | bytes 4194304
  44.7 11.3 %slice-start.1 = ((s8[6291456]{0:T(1024)(128)(4,1)}), s8[4194304]{0:T(1024)(128)(4,1)S(1)}, s32[]{:S(2)}) async-start(s8[6291456]{0:T(1024)(128)(4,1)} %bitcast.108), calls=%async_computation.3 | async-start | bytes 8388608
  48.7 231.2 %collective-permute-start.1 = (bf16[2048,768]{1,0:T(8,128)(2,1)}, bf16[2048,768]{1,0:T(8,128)(2,1)}, u32[]{:S(2)}, u32[]{:S(2)}) collective-permute-start(bf16[2048,768]{1,0:T(8,128)(2,1)} %dynamic-slice_bitcast_fusion.1), channel_id=1, source_target_pairs={{0,1},{1,2},{2,3},{3,4},{4,5},{5,6},{6,7},{7,8},{8,9},{9,10},{10,1... | collective-permute-start | bytes 9437192 | tf_op jit(solution)/shard_map/ppermute | solution.py:10
  54.4 293.0 %collective-permute-start = (bf16[2048,768]{1,0:T(8,128)(2,1)}, bf16[2048,768]{1,0:T(8,128)(2,1)}, u32[]{:S(2)}, u32[]{:S(2)}) collective-permute-start(bf16[2048,768]{1,0:T(8,128)(2,1)} %dynamic-slice_bitcast_fusion.2), channel_id=1, source_target_pairs={{0,1},{1,2},{2,3},{3,4},{4,5},{5,6},{6,7},{7,8},{8,9},{9,10},{10,1... | collective-permute-start | bytes 9437192 | tf_op jit(solution)/shard_map/ppermute | solution.py:10
  57.8 355.7 %collective-permute-start.2 = (bf16[768,2048]{1,0:T(8,128)(2,1)}, bf16[768,2048]{1,0:T(8,128)(2,1)}, u32[]{:S(2)}, u32[]{:S(2)}) collective-permute-start(bf16[768,2048]{1,0:T(8,128)(2,1)} %dynamic-slice_bitcast_fusion), channel_id=1, source_target_pairs={{0,1},{1,2},{2,3},{3,4},{4,5},{5,6},{6,7},{7,8},{8,9},{9,10},{10,1... | collective-permute-start | bytes 9437192 | tf_op jit(solution)/shard_map/ppermute | solution.py:10
  437.6 22.5 %copy-start.2 = (f32[256,8]{0,1:T(8,128)S(1)}, f32[256,8]{0,1:T(8,128)}, u32[]{:S(2)}) copy-start(f32[256,8]{0,1:T(8,128)} %param.9) | copy-start | bytes 24580
  437.6 205.2 %all-to-all-start.1 = ((bf16[16,3,64,2048]{3,2,1,0:T(8,128)(2,1)}), bf16[16,3,64,2048]{3,2,1,0:T(8,128)(2,1)}, u32[]{:S(2)}, u32[]{:S(2)}) async-start(bf16[16,3,64,2048]{3,2,1,0:T(8,128)(2,1)} %copy.25), calls=%async_computation.1 | async-start | bytes 25165824 | tf_op jit(solution)/shard_map/all_to_all | solution.py:50
  642.8 34.9 %copy-start.1 = (bf16[256,2048]{1,0:T(8,128)(2,1)S(1)}, bf16[256,2048]{1,0:T(8,128)(2,1)}, u32[]{:S(2)}) copy-start(bf16[256,2048]{1,0:T(8,128)(2,1)} %param.7) | copy-start | bytes 3145732
where the time goes:
time: 687 us; the launch traced here: 678 us
  waiting for transfers between devices  494 us (72%)
  local copies, waits for them, and re-layouts  58.5 us (9%)
  matrix products  56.6 us (8%)
  starting transfers between devices  35.2 us (5%)
  other arithmetic  32.6 us (5%)
    all_to_all x1, waiting for transfers between devices, body(): lax.all_to_all(results, 'expert', split_axis=0, concat_axis=0, tiled=True)  183 us
    all_to_all x1, waiting for transfers between devices, body(): lax.all_to_all(outgoing, 'expert', split_axis=0, concat_axis=0, tiled=True)  173 us
    ppermute x3, waiting for transfers between devices, shifted(): return lax.ppermute(value, axis, pairs)  138 us
    gather x1, local copies, waits for them, and re-layouts, body(): returned.reshape(virtual * capacity, width)[row_index]  22.6 us
    all_to_all x1, starting transfers between devices, body(): lax.all_to_all(results, 'expert', split_axis=0, concat_axis=0, tiled=True)  22.5 us
    dot_general x1, matrix products, body(): jnp.einsum('nscf,sfd->nscd', hidden, w_down, preferred_element_type=jnp.f...  22.2 us
    scatter x1, local copies, waits for them, and re-layouts, body(): buffer.at[row_index]  19.1 us
    another operation x3, other arithmetic  14 us
  transfers between devices with their start and end apart: 5, of which 5 were waited for; matrix products, arithmetic and copies ran while one was open for 8% of the time, Pallas kernels for 0%

commit v1 on v0

v1 whole, which is shorter than its diff:
```python
import jax
import jax.numpy as jnp
from jax import lax
from jax.sharding import PartitionSpec as P


def body(tokens, target, router_weight, replica_pick, w_gate, w_up, w_down):
    tok_rows, width = tokens.shape
    per_device = w_gate.shape[0]
    slots = per_device + 1
    groups = lax.axis_size("expert")
    me = lax.axis_index("expert")
    share = router_weight / jnp.sum(router_weight, axis=1, keepdims=True)
    all_tokens = lax.all_gather(tokens, "expert", axis=0, tiled=True)
    all_target = lax.all_gather(target, "expert", axis=0, tiled=True)
    all_share = lax.all_gather(share, "expert", axis=0, tiled=True)
    lent = replica_pick[0]
    away = lax.rem(me + 1, groups) * slots + per_device
    parts = []
    for local in range(per_device):
        hit = all_target == me * slots + local
        hit = hit | ((all_target == away) & (lent == local))
        coeff = jnp.sum(jnp.where(hit, all_share, 0.0), axis=1, keepdims=True)
        gate = jnp.dot(all_tokens, w_gate[local], preferred_element_type=jnp.float32)
        upper = jnp.dot(all_tokens, w_up[local], preferred_element_type=jnp.float32)
        parts.append((jax.nn.silu(gate) * upper * coeff).astype(jnp.bfloat16))
    hidden = jnp.concatenate(parts, axis=1)
    down = w_down.reshape(-1, width)
    partial = jnp.dot(hidden, down, preferred_element_type=jnp.float32).astype(jnp.bfloat16)
    return lax.psum_scatter(partial, "expert", scatter_dimension=0, tiled=True)


def solution(mesh):
    in_specs = (
        P(("dp", "expert"), None),
        P(("dp", "expert"), None),
        P(("dp", "expert"), None),
        P(("dp", "expert")),
        P("expert", None, None),
        P("expert", None, None),
        P("expert", None, None),
    )
    out_specs = P(("dp", "expert"), None)
    return jax.shard_map(body, mesh=mesh, in_specs=in_specs, out_specs=out_specs, check_vma=False)
```

time: 687 us -> 363 us (0.53); the launches traced: 678 us -> 363 us
  waiting for transfers between devices: 494 us -> 177 us
  matrix products: 56.6 us -> 121 us
  local copies, waits for them, and re-layouts: 58.5 us -> 0 us
  blocking collectives: 0 us -> 49.3 us
  starting transfers between devices: 35.2 us -> 0.04 us
  other arithmetic: 32.6 us -> 1.54 us
  between operations: 1.18 us -> 14.1 us
    all_to_all x2 -> x0, waiting for transfers between devices: 356 us -> none  [the longest x1 183 us: body(): lax.all_to_all(results, 'expert', split_axis=0, concat_axis=0, tiled=True)]
    ppermute x3 -> x0, waiting for transfers between devices: 138 us -> none  [shifted(): return lax.ppermute(value, axis, pairs)]
    reduce_scatter x0 -> x1, waiting for transfers between devices: none -> 111 us  [body(): return lax.psum_scatter(partial, 'expert', scatter_dimension=0, tiled=True)]
    all_gather x0 -> x1, waiting for transfers between devices: none -> 65.1 us  [body(): all_tokens = lax.all_gather(tokens, 'expert', axis=0, tiled=True)]
    dot_general x4 -> x5, matrix products: 56.6 us -> 121 us  [the longest x2 47.6 us: body(): upper = jnp.dot(all_tokens, w_up[local], preferred_element_type=jnp.float32)]
    all_gather x0 -> x2, blocking collectives: none -> 49.3 us  [the longest x1 25.8 us: body(): all_share = lax.all_gather(share, 'expert', axis=0, tiled=True)]
    all_to_all x2 -> x0, starting transfers between devices: 30.6 us -> none  [the longest x1 22.5 us: body(): lax.all_to_all(results, 'expert', split_axis=0, concat_axis=0, tiled=True)]
    gather x1 -> x0, local copies, waits for them, and re-layouts: 22.6 us -> none  [body(): returned.reshape(virtual * capacity, width)[row_index]]
  transfers between devices with their start and end apart: 5 -> 2, of which waited for: 5 -> 2; matrix products, arithmetic and copies ran while one was open for 8% -> 0% of each run, Pallas kernels for 0% -> 0%
where the time goes in v1:
time: 363 us
  waiting for transfers between devices  177 us (49%)
  matrix products  121 us (33%)
  blocking collectives  49.3 us (14%)
  between operations  14.1 us (4%)
    reduce_scatter x1, waiting for transfers between devices, body(): return lax.psum_scatter(partial, 'expert', scatter_dimension=0, tiled=True)  111 us
    all_gather x1, waiting for transfers between devices, body(): all_tokens = lax.all_gather(tokens, 'expert', axis=0, tiled=True)  65.1 us
    dot_general x2, matrix products, body(): upper = jnp.dot(all_tokens, w_up[local], preferred_element_type=jnp.float32)  47.6 us
    dot_general x2, matrix products, body(): jnp.dot(all_tokens, w_gate[local], preferred_element_type=jnp.float32)  40.7 us
    dot_general x1, matrix products, body(): jnp.dot(hidden, down, preferred_element_type=jnp.float32)  32.9 us
    all_gather x1, blocking collectives, body(): all_share = lax.all_gather(share, 'expert', axis=0, tiled=True)  25.8 us
    all_gather x1, blocking collectives, body(): all_target = lax.all_gather(target, 'expert', axis=0, tiled=True)  23.6 us
  transfers between devices with their start and end apart: 2, of which 2 were waited for; matrix products, arithmetic and copies ran while one was open for 0% of the time, Pallas kernels for 0%

profile of v1, /device:TPU:0, one launch (start us, length us, event | category | flops | bytes accessed | tf_op | source)
XLA Modules:
  0.0 362.8 jit_solution(1969170767023350826)
XLA Ops:
  6.5 0.0 all-gather.2.cloned.1.call-start
  6.5 0.7 all-gather.2.cloned.1.call-update
  7.3 0.0 reduce-scatter.2.cloned.1.call-start
  8.0 0.7 reduce_sum.27
  8.7 0.7 broadcast_divide_fusion
  9.4 25.8 %all_gather.11 = f32[4096,8]{0,1:T(8,128)S(1)} all-gather(f32[256,8]{0,1:T(8,128)S(1)} %broadcast_divide_fusion), channel_id=1, replica_groups=mesh['dp'=8,'expert'=16] {'expert'}, dimensions={0}, use_global_device_ids=true | all-gather | bytes 139264 | tf_op jit(solution)/shard_map/all_gather | solution.py:16
  35.2 23.6 %all_gather.10 = s32[4096,8]{0,1:T(8,128)S(1)} all-gather(s32[256,8]{0,1:T(8,128)} %param.8), channel_id=1, replica_groups=mesh['dp'=8,'expert'=16] {'expert'}, dimensions={0}, use_global_device_ids=true | all-gather | bytes 139264 | tf_op jit(solution)/shard_map/all_gather | solution.py:15
  58.7 0.1 select_reduce_fusion.1
  58.8 65.1 %all-gather.2.cloned.1.call-done = bf16[4096,2048]{1,0:T(8,128)(2,1)} async-done(((bf16[256,2048]{1,0:T(8,128)(2,1)}), bf16[4096,2048]{1,0:T(8,128)(2,1)}) %all-gather.2.cloned.1.call-update) | async-done | bytes 16777232 | tf_op jit(solution)/shard_map/all_gather | solution.py:14
  124.0 20.3 %fusion.4 = f32[4096,768]{0,1:T(8,128)} fusion(bf16[4096,2048]{1,0:T(8,128)(2,1)} %all-gather.2.cloned.1.call-done, bf16[2,2048,768]{2,1,0:T(8,128)(2,1)} %param.11), kind=kOutput, calls=%fused_computation.7 | convolution fusion | flops 12884901888 | bytes 32505856 | tf_op jit(solution)/shard_map/dot_general | solution.py:24
  144.3 20.4 %fusion.7 = f32[4096,768]{0,1:T(8,128)} fusion(bf16[4096,2048]{1,0:T(8,128)(2,1)} %all-gather.2.cloned.1.call-done, bf16[2,2048,768]{2,1,0:T(8,128)(2,1)} %param.11), kind=kOutput, calls=%fused_computation.10 | convolution fusion | flops 12884901888 | bytes 32505856 | tf_op jit(solution)/shard_map/dot_general | solution.py:24
  164.7 23.8 %multiply_convert_fusion = bf16[4096,768]{0,1:T(8,128)(2,1)} fusion(f32[4096,768]{0,1:T(8,128)} %fusion.4, bf16[4096,2048]{1,0:T(8,128)(2,1)} %all-gather.2.cloned.1.call-done, f32[4096]{0:T(1024)S(1)} %get-tuple-element.6, bf16[2,2048,768]{2,1,0:T(8,128)(2,1)} %param.12), kind=kOutput, calls=%fused_computation.4 | convolution fusion | flops 12906921984 | bytes 38813696 | tf_op jit(solution)/shard_map/dot_general | solution.py:25
  188.4 23.8 %multiply_convert_fusion.1 = bf16[4096,768]{0,1:T(8,128)(2,1)} fusion(f32[4096,768]{0,1:T(8,128)} %fusion.7, bf16[4096,2048]{1,0:T(8,128)(2,1)} %all-gather.2.cloned.1.call-done, f32[4096]{0:T(1024)S(1)} %get-tuple-element.5, bf16[2,2048,768]{2,1,0:T(8,128)(2,1)} %param.12), kind=kOutput, calls=%fused_computation.5 | convolution fusion | flops 12906921984 | bytes 38813696 | tf_op jit(solution)/shard_map/dot_general | solution.py:25
  212.2 32.9 %convolution_convert_fusion = bf16[4096,2048]{1,0:T(8,128)(2,1)} fusion(bf16[1536,2048]{1,0:T(8,128)(2,1)} %bitcast.20, bf16[4096,768]{0,1:T(8,128)(2,1)} %multiply_convert_fusion, bf16[4096,768]{0,1:T(8,128)(2,1)} %multiply_convert_fusion.1), kind=kOutput, calls=%fused_computation | convolution fusion | flops 25803358208 | bytes 35651584 | tf_op jit(solution)/shard_map/dot_general | solution.py:29
  245.2 0.0 reduce-scatter.2.cloned.1.call-update
  245.2 110.8 %reduce-scatter.2.cloned.1.call-done = bf16[256,2048]{1,0:T(8,128)(2,1)} async-done(((bf16[4096,2048]{1,0:T(8,128)(2,1)}), bf16[256,2048]{1,0:T(8,128)(2,1)}) %reduce-scatter.2.cloned.1.call-update) | async-done | bytes 1048592 | tf_op jit(solution)/shard_map/reduce_scatter | solution.py:30
Async XLA Ops:
  6.5 117.4 %all-gather.2.cloned.1.call-start = ((), (), s32[]{:S(2)}) async-start(), calls=%async_computation.1 | async-start | bytes 17825792 | tf_op jit(solution)/shard_map/all_gather | solution.py:14
  7.3 348.7 %reduce-scatter.2.cloned.1.call-start = ((), (), s32[]{:S(2)}) async-start(), calls=%async_computation.2 | async-start | bytes 17825792 | tf_op jit(solution)/shard_map/reduce_scatter | solution.py:30
Sparse Core Ops, SparseCore 0:
  9.5 114.4 all-gather.1
  245.3 110.6 reduce-scatter.1

commit v2 on v1

v2 whole, which is shorter than its diff:
```python
import functools

import jax
import jax.numpy as jnp
from jax import lax
from jax.experimental import pallas as pl
from jax.experimental.pallas import tpu as pltpu
from jax.sharding import PartitionSpec as P

SIDE = 4
CHUNKS = 2
GROUP = 4
DIRS = ((0, 1), (0, -1), (1, 0), (-1, 0))
K1, K2, K3, K4A, K4B, K5, K7, K6A, K6B, K8 = range(10)
FULL = {K1: 0, K2: 1, K4A: 2, K4B: 3, K7: 4}
HALF = {K3: 0, K5: 1, K6A: 2, K6B: 3, K8: 4}
ORDER = (
    (0, 0), (0, 1), (0, 3), (1, 0),
    (3, 0), (1, 1), (1, 3), (3, 1),
    (3, 3), (0, 2), (2, 0), (1, 2),
    (3, 2), (2, 1), (2, 3), (2, 2),
)
WHERE = {offset: place for place, offset in enumerate(ORDER)}


def plus(a, b, scale=1):
    return ((a[0] + scale * b[0]) % SIDE, (a[1] + scale * b[1]) % SIDE)


def block_of(kind, d, rows):
    along_x = d[0] == 0
    first = 0 if along_x else 1
    other = 1 - first
    w = (1, 0) if along_x else (0, 1)
    zero = (0, 0)
    back = plus(zero, d, -1)
    whole = (0, rows)
    part = (0, rows // 2) if d[0] + d[1] > 0 else (rows // 2, rows // 2)
    return {
        K1: (first, zero, whole),
        K2: (other, zero, whole),
        K3: (first, back, part),
        K4A: (other, plus(zero, w), whole),
        K4B: (other, plus(zero, w, -1), whole),
        K5: (other, back, part),
        K7: (other, plus(zero, w, 2), whole),
        K6A: (other, plus(w, d, -1), part),
        K6B: (other, plus(plus(zero, w, -1), d, -1), part),
        K8: (other, plus(plus(zero, w, 2), d, -1), part),
    }[kind]


def kernel(
    tokens, target, weight, lent, w_gate, w_up, w_down, out,
    buf, wg, wu, wd, hid, coef, sh_out, sh_in, rfull, rhalf,
    wsem, tsem, osem, ag_send, ag_recv, rs_send, rs_recv, sh_send, sh_recv,
):
    dp = lax.axis_index("dp")
    me = lax.axis_index("expert")
    my_z, my_x = me // SIDE, me % SIDE
    experts, width, ff = w_gate.shape
    rows = tokens.shape[0] // CHUNKS
    half = width // 2
    tile = 256 if ff % 256 == 0 else 128
    wide = 512 if width % 512 == 0 else 128
    hidden_tiles = experts * ff // tile
    out_tiles = width // wide
    steps = hidden_tiles + out_tiles
    group_rows = GROUP * rows
    groups = CHUNKS * len(ORDER) // GROUP

    def at(offset):
        z = lax.rem(my_z + offset[0] + SIDE, SIDE)
        x = lax.rem(my_x + offset[1] + SIDE, SIDE)
        return z * SIDE + x

    def device(offset):
        return (dp, at(offset))

    def region(b, h, offset, part):
        start = WHERE[offset] * rows + part[0]
        return buf.at[b, pl.ds(start, part[1]), pl.ds(h * half, half)]

    def gather_copy(c, kind, n):
        d = DIRS[n]
        h, q, part = block_of(kind, d, rows)
        return pltpu.make_async_remote_copy(
            src_ref=region(c, h, q, part),
            dst_ref=region(c, h, plus(q, d, -1), part),
            send_sem=ag_send.at[c, kind, n],
            recv_sem=ag_recv.at[c, kind, n],
            device_id=device(d),
            device_id_type=pl.DeviceIdType.MESH,
        )

    def landing(c, kind, n):
        if kind in FULL:
            return rfull.at[c, FULL[kind], n]
        return rhalf.at[c, HALF[kind], n]

    def sum_buffer(c):
        return 2 - 2 * c

    def reduce_copy(c, kind, n):
        d = DIRS[n]
        h, q, part = block_of(kind, d, rows)
        return pltpu.make_async_remote_copy(
            src_ref=region(sum_buffer(c), h, plus(q, d, -1), part),
            dst_ref=landing(c, kind, n),
            send_sem=rs_send.at[c, kind, n],
            recv_sem=rs_recv.at[c, kind, n],
            device_id=device((-d[0], -d[1])),
            device_id_type=pl.DeviceIdType.MESH,
        )

    def start(make, c, kinds):
        for kind in kinds:
            for n in range(4):
                make(c, kind, n).start()

    def arrive(make, c, kinds):
        for kind in kinds:
            for n in range(4):
                make(c, kind, n).wait_recv()

    def sent(make, c):
        for kind in range(10):
            for n in range(4):
                make(c, kind, n).wait_send()

    def add(c, pairs):
        where = {}
        for kind, n in pairs:
            h, q, part = block_of(kind, DIRS[n], rows)
            where.setdefault((h, q, part), []).append(landing(c, kind, n))
        b = sum_buffer(c)
        for (h, q, part), sources in where.items():
            base = WHERE[q] * rows + part[0]
            cols = pl.ds(h * half, half)

            @pl.loop(0, part[1] // 16)
            def _(r):
                spot = pl.ds(pl.multiple_of(base + r * 16, 16), 16)
                total = buf[b, spot, cols].astype(jnp.float32)
                for source in sources:
                    total += source[pl.ds(pl.multiple_of(r * 16, 16), 16), :].astype(jnp.float32)
                buf[b, spot, cols] = total.astype(jnp.bfloat16)

    everywhere = range(4)

    def each(*kinds):
        return [(kind, n) for kind in kinds for n in everywhere]

    def ag(c, stage):
        if stage == 0:
            start(gather_copy, c, (K1, K2))
        elif stage == 1:
            arrive(gather_copy, c, (K1,))
            start(gather_copy, c, (K3, K4A, K4B))
        elif stage == 2:
            arrive(gather_copy, c, (K2,))
            start(gather_copy, c, (K5,))
        elif stage == 3:
            arrive(gather_copy, c, (K3,))
            start(gather_copy, c, (K7,))
        elif stage == 4:
            arrive(gather_copy, c, (K4A, K4B))
            start(gather_copy, c, (K6A, K6B))
        elif stage == 5:
            arrive(gather_copy, c, (K5,))
        elif stage == 6:
            arrive(gather_copy, c, (K7,))
            start(gather_copy, c, (K8,))
        elif stage == 7:
            arrive(gather_copy, c, (K6A, K6B))
        elif stage == 8:
            arrive(gather_copy, c, (K8,))

    def rs(c, stage):
        if stage == 0:
            start(reduce_copy, c, (K8, K6A, K6B, K5))
        elif stage == 1:
            arrive(reduce_copy, c, (K8,))
            add(c, each(K8))
            start(reduce_copy, c, (K7,))
        elif stage == 2:
            arrive(reduce_copy, c, (K6A, K6B))
            add(c, each(K6A, K6B))
            start(reduce_copy, c, (K4A, K4B))
        elif stage == 3:
            arrive(reduce_copy, c, (K5,))
            add(c, each(K5))
            start(reduce_copy, c, (K2,))
        elif stage == 4:
            arrive(reduce_copy, c, (K7,))
            add(c, each(K7))
            start(reduce_copy, c, (K3,))
        elif stage == 5:
            arrive(reduce_copy, c, (K4A, K4B))
            add(c, each(K4A, K4B))
        elif stage == 6:
            arrive(reduce_copy, c, (K3,))
            add(c, each(K3))
            start(reduce_copy, c, (K1,))
        elif stage == 7:
            arrive(reduce_copy, c, (K2, K1))
            add(c, each(K2, K1))
            result(c).start()

    def result(c):
        return pltpu.make_async_copy(
            buf.at[sum_buffer(c), pl.ds(0, rows), :], out.at[pl.ds(c * rows, rows), :], osem.at[c]
        )

    def own(c):
        return pltpu.make_async_copy(
            tokens.at[pl.ds(c * rows, rows), :], buf.at[c, pl.ds(0, rows), :], tsem.at[c]
        )

    def weights():
        copies = []
        for e in range(experts):
            span = pl.ds(e * ff, ff)
            copies.append(pltpu.make_async_copy(w_gate.at[e], wg.at[:, span], wsem.at[0, e]))
            copies.append(pltpu.make_async_copy(w_up.at[e], wu.at[:, span], wsem.at[1, e]))
            copies.append(pltpu.make_async_copy(w_down.at[e], wd.at[span, :], wsem.at[2, e]))
        return copies

    def share_copy(offset):
        back = plus((0, 0), offset, -1)
        return pltpu.make_async_remote_copy(
            src_ref=sh_out.at[WHERE[offset]],
            dst_ref=sh_in.at[WHERE[back]],
            send_sem=sh_send.at[WHERE[offset]],
            recv_sem=sh_recv.at[WHERE[back]],
            device_id=device(offset),
            device_id_type=pl.DeviceIdType.MESH,
        )

    def share_arrival(offset):
        return share_copy(plus((0, 0), offset, -1))

    for c in range(CHUNKS):
        own(c).start()
    barrier = pltpu.get_barrier_semaphore()
    for offset in ORDER[1:]:
        pl.semaphore_signal(
            barrier, inc=1, device_id=device(offset), device_id_type=pl.DeviceIdType.MESH
        )
    choice = target[...]
    share = weight[...]
    share = share / jnp.sum(share, axis=0, keepdims=True)
    slots = experts + 1
    count = SIDE * SIDE
    for offset in ORDER:
        host = at(offset)
        named = [host * slots + k for k in range(experts)] + [lax.rem(host + 1, count) * slots + experts]
        for k, slot in enumerate(named):
            sh_out[WHERE[offset], k:k + 1, :] = jnp.sum(
                jnp.where(choice == slot, share, 0.0), axis=0, keepdims=True
            )
        for k in range(len(named), 8):
            sh_out[WHERE[offset], k:k + 1, :] = jnp.zeros((1, share.shape[1]), jnp.float32)
    for c in range(CHUNKS):
        own(c).wait()
    pl.semaphore_wait(barrier, len(ORDER) - 1)
    ag(0, 0)
    for copy in weights():
        copy.start()
    for offset in ORDER[1:]:
        share_copy(offset).start()
    sh_in[0] = sh_out[0]
    ag(0, 1)
    for offset in ORDER[1:]:
        share_arrival(offset).wait_recv()
    second = lent[0:1, :]
    for c in range(CHUNKS):
        span = pl.ds(c * rows, rows)
        for p in range(len(ORDER)):
            spare = sh_in[p, 2:3, span]
            sh_in[p, 0:1, span] = sh_in[p, 0:1, span] + (1.0 - second) * spare
            sh_in[p, 1:2, span] = sh_in[p, 1:2, span] + second * spare
        table = jnp.concatenate([sh_in[p, :, span] for p in range(len(ORDER))], axis=0)
        turned = jnp.transpose(table)
        for p in range(len(ORDER)):
            coef[pl.ds((c * len(ORDER) + p) * rows, rows), :] = turned[:, p * 8:p * 8 + 8]
    ag(0, 2)
    for copy in weights():
        copy.wait()

    events = {}

    def plan(g, j, fn, *args):
        events.setdefault(g * steps + min(j, steps - 1), []).append((fn, args))

    plan(0, 2, ag, 0, 3)
    plan(1, 0, ag, 0, 4)
    plan(1, 3, ag, 0, 5)
    plan(1, 8, ag, 0, 6)
    plan(1, 8, ag, 1, 0)
    plan(2, 0, ag, 0, 7)
    plan(2, 3, ag, 0, 8)
    plan(2, 8, ag, 1, 1)
    plan(3, 2, ag, 1, 2)
    plan(3, 4, ag, 1, 3)
    plan(4, 3, ag, 1, 4)
    plan(4, 6, sent, gather_copy, 0)
    plan(4, 6, ag, 1, 5)
    plan(5, 1, ag, 1, 6)
    plan(5, 1, rs, 0, 0)
    plan(5, 5, ag, 1, 7)
    plan(5, 8, ag, 1, 8)
    plan(6, 1, rs, 0, 1)
    plan(6, 5, rs, 0, 2)
    plan(6, 8, rs, 0, 3)
    plan(7, 2, rs, 0, 4)

    @pl.loop(0, groups * steps)
    def _(i):
        for when, calls in events.items():
            @pl.when(i == when)
            def _(calls=calls):
                for fn, args in calls:
                    fn(*args)
        g = i // steps
        j = i % steps
        c = g // (groups // CHUNKS)
        row0 = pl.multiple_of((g % (groups // CHUNKS)) * group_rows, group_rows)

        @pl.when(j < hidden_tiles)
        def _():
            cols = pl.ds(pl.multiple_of(j * tile, tile), tile)
            x = buf[c, pl.ds(row0, group_rows), :]
            gate = jnp.dot(x, wg[:, cols], preferred_element_type=jnp.float32)
            upper = jnp.dot(x, wu[:, cols], preferred_element_type=jnp.float32)
            both = coef[pl.ds(pl.multiple_of(g * group_rows, group_rows), group_rows), :]
            scale = jnp.where(j < hidden_tiles // experts, both[:, 0:1], both[:, 1:2])
            value = gate / (1.0 + jnp.exp(-gate)) * upper * scale
            hid[:, cols] = value.astype(jnp.bfloat16)

        @pl.when(j >= hidden_tiles)
        def _():
            cols = pl.ds(pl.multiple_of((j - hidden_tiles) * wide, wide), wide)
            y = jnp.dot(hid[...], wd[:, cols], preferred_element_type=jnp.float32)
            buf[2 - 2 * c, pl.ds(row0, group_rows), cols] = y.astype(jnp.bfloat16)

    rs(1, 0)
    rs(0, 5)
    rs(0, 6)
    rs(1, 1)
    rs(1, 2)
    rs(1, 3)
    rs(0, 7)
    rs(1, 4)
    rs(1, 5)
    rs(1, 6)
    rs(1, 7)
    for c in range(CHUNKS):
        result(c).wait()
    sent(gather_copy, 1)
    sent(reduce_copy, 0)
    sent(reduce_copy, 1)
    for offset in ORDER[1:]:
        share_copy(offset).wait_send()


def body(tokens, target, router_weight, replica_pick, w_gate, w_up, w_down):
    tok_rows, width = tokens.shape
    experts, _, ff = w_gate.shape
    rows = tok_rows // CHUNKS
    count = SIDE * SIDE
    lent = jnp.broadcast_to(replica_pick.astype(jnp.float32)[:, None], (8, rows))
    any_space = pl.BlockSpec(memory_space=pl.ANY)
    vmem = pl.BlockSpec(memory_space=pltpu.VMEM)
    dma = pltpu.SemaphoreType.DMA
    moved = 30 * rows * width
    return pl.pallas_call(
        kernel,
        out_shape=jax.ShapeDtypeStruct((tok_rows, width), jnp.bfloat16),
        in_specs=[any_space, vmem, vmem, vmem, any_space, any_space, any_space],
        out_specs=any_space,
        scratch_shapes=[
            pltpu.VMEM((3, count * rows, width), jnp.bfloat16),
            pltpu.VMEM((width, experts * ff), jnp.bfloat16),
            pltpu.VMEM((width, experts * ff), jnp.bfloat16),
            pltpu.VMEM((experts * ff, width), jnp.bfloat16),
            pltpu.VMEM((GROUP * rows, experts * ff), jnp.bfloat16),
            pltpu.VMEM((count * tok_rows, 8), jnp.float32),
            pltpu.VMEM((count, 8, tok_rows), jnp.float32),
            pltpu.VMEM((count, 8, tok_rows), jnp.float32),
            pltpu.VMEM((CHUNKS, len(FULL), 4, rows, width // 2), jnp.bfloat16),
            pltpu.VMEM((CHUNKS, len(HALF), 4, rows // 2, width // 2), jnp.bfloat16),
            dma((3, experts)),
            dma((CHUNKS,)),
            dma((CHUNKS,)),
            dma((CHUNKS, 10, 4)),
            dma((CHUNKS, 10, 4)),
            dma((CHUNKS, 10, 4)),
            dma((CHUNKS, 10, 4)),
            dma((count,)),
            dma((count,)),
        ],
        compiler_params=pltpu.CompilerParams(
            collective_id=0, has_side_effects=True, vmem_limit_bytes=67043328
        ),
        cost_estimate=pl.CostEstimate(
            flops=6 * count * tok_rows * width * ff * experts,
            bytes_accessed=3 * experts * width * ff * 2,
            transcendentals=count * tok_rows * ff * experts,
        ),
        name="moe_layer",
    )(tokens, target.T, router_weight.T, lent, w_gate, w_up, w_down)


def solution(mesh):
    in_specs = (
        P(("dp", "expert"), None),
        P(("dp", "expert"), None),
        P(("dp", "expert"), None),
        P(("dp", "expert")),
        P("expert", None, None),
        P("expert", None, None),
        P("expert", None, None),
    )
    out_specs = P(("dp", "expert"), None)
    return jax.shard_map(body, mesh=mesh, in_specs=in_specs, out_specs=out_specs, check_vma=False)
```

time: 363 us -> 198 us (0.55)
  Pallas kernels: 0 us -> 194 us
  waiting for transfers between devices: 177 us -> 0 us
  matrix products: 121 us -> 0 us
  blocking collectives: 49.3 us -> 0 us
  between operations: 14.1 us -> 0.66 us
    pallas_call x0 -> x1, Pallas kernels: none -> 194 us  [body(): pl.pallas_call(kernel, out_shape=jax.ShapeDtypeStruct((tok_rows, width),...]
    dot_general x5 -> x0, matrix products: 121 us -> none  [the longest x2 47.6 us: body(): upper = jnp.dot(all_tokens, w_up[local], preferred_element_type=jnp.float32)]
    reduce_scatter x1 -> x0, waiting for transfers between devices: 111 us -> none  [body(): return lax.psum_scatter(partial, 'expert', scatter_dimension=0, tiled=True)]
    all_gather x1 -> x0, waiting for transfers between devices: 65.1 us -> none  [body(): all_tokens = lax.all_gather(tokens, 'expert', axis=0, tiled=True)]
    all_gather x2 -> x0, blocking collectives: 49.3 us -> none  [the longest x1 25.8 us: body(): all_share = lax.all_gather(share, 'expert', axis=0, tiled=True)]
  transfers between devices with their start and end apart: 2 -> 0, of which waited for: 2 -> 0; matrix products, arithmetic and copies ran while one was open for 0% -> 0% of each run, Pallas kernels for 0% -> 0%
where the time goes in v2:
time: 198 us
  Pallas kernels  194 us (98%)
  local copies, waits for them, and re-layouts  2.9 us (1%)
    pallas_call x1, Pallas kernels, body(): pl.pallas_call(kernel, out_shape=jax.ShapeDtypeStruct((tok_rows, width),...  194 us

profile of v2, /device:TPU:0, one launch (start us, length us, event | category | flops | bytes accessed | tf_op | source)
XLA Modules:
  0.0 197.8 jit_solution(9766822199242880124)
XLA Ops:
  0.7 0.6 broadcast_in_dim.9.lent
  1.2 194.2 %moe_layer.1 = bf16[256,2048]{1,0:T(8,128)(2,1)} custom-call(bf16[256,2048]{1,0:T(8,128)(2,1)} %tokens.1, s32[8,256]{1,0:T(8,128)} %bitcast.3, f32[8,256]{1,0:T(8,128)} %bitcast.4, f32[8,128]{1,0:T(8,128)} %broadcast_in_dim.9.lent, bf16[2,2048,768]{2,1,0:T(8,128)(2,1)} %w_gate.1, bf16[2,2048,768]{2,1,0:T(8,128)(2,1)} %w_up.1, bf16[2,768,2048]{2,1,0:T(8,128)(2,1)} %w_down.1), custom_call_target="tpu_custom_call" | custom-call | flops 77309411328 | bytes 18874368 | tf_op jit(solution)/shard_map/moe_layer/pallas_call | solution.py:377
  195.5 2.3 %copy.10 = bf16[256,2048]{1,0:T(8,128)(2,1)} copy(bf16[256,2048]{1,0:T(8,128)(2,1)} %moe_layer.1) | data formatting | bytes 2097152

commit v3 on v1

v3 whole, which is shorter than its diff:
```python
import jax
import jax.numpy as jnp
from jax import lax
from jax.experimental import pallas as pl
from jax.experimental.pallas import tpu as pltpu
from jax.sharding import PartitionSpec as P

SIDE = 4
CHUNKS = 4
ORDER = tuple((dz, s) for s in range(2) for dz in range(SIDE))
WHERE = {offset: place for place, offset in enumerate(ORDER)}
UP, DOWN, OUTER = range(3)
STEP = {UP: 1, DOWN: -1}
Z_KINDS = ("Z1A", "Z1B", "Z2", "Z3A", "Z3B", "Z4")
O_KINDS = ("O1A", "O1B", "O3", "O4", "O5")
COPIES = tuple((k, n) for k in Z_KINDS for n in (UP, DOWN)) + tuple((k, OUTER) for k in O_KINDS)
INDEX = {copy: i for i, copy in enumerate(COPIES)}


def block_of(kind, n):
    if n == OUTER:
        return {
            "O1A": ("A", (0, 0), None), "O1B": ("B", (0, 0), None), "O3": ("B", (1, 0), None),
            "O4": ("B", (3, 0), None), "O5": ("B", (2, 0), None),
        }[kind]
    back = -STEP[n] % SIDE
    return {
        "Z1A": ("A", (0, 0), None), "Z1B": ("B", (0, 0), None), "Z2": ("A", (0, 1), None),
        "Z3A": ("A", (back, 0), n), "Z3B": ("B", (back, 0), n), "Z4": ("A", (back, 1), n),
    }[kind]


def moved(offset, n):
    if n == OUTER:
        return (offset[0], 1 - offset[1])
    return ((offset[0] - STEP[n]) % SIDE, offset[1])


SIZES = {}
SPOT = {}
for _copy in COPIES:
    _cols, _, _part = block_of(*_copy)
    _key = (_cols, _part is not None)
    SPOT[_copy] = (_key, SIZES.get(_key, 0))
    SIZES[_key] = SIZES.get(_key, 0) + 1
LANDINGS = tuple(sorted(SIZES))


def kernel(
    tokens, target, weight, lent, w_gate, w_up, w_down, out,
    buf, wg, wu, wd, hid, hid_two, coef, sh_out, sh_in, lent_in, land_a, land_b, land_c, land_d,
    wsem, tsem, osem, ag_send, ag_recv, rs_send, rs_recv, sh_send, sh_recv, ln_send, ln_recv,
    x_send, x_recv, y_send, y_recv, r_send, r_recv, c_send, c_recv,
):
    dp = lax.axis_index("dp")
    me = lax.axis_index("expert")
    my_z, my_x = me // SIDE, me % SIDE
    my_y, my_core = dp // 2, dp % 2
    experts, width, ff = w_gate.shape
    own = experts * ff
    rows = tokens.shape[0] // CHUNKS
    group = rows * len(ORDER)
    split = width // 128 * 9 // 16 * 128
    columns = {"A": (0, split), "B": (split, width - split)}
    landings = dict(zip(LANDINGS, (land_a, land_b, land_c, land_d)))
    tile = 256 if ff % 256 == 0 else 128
    wide = 512 if width % 512 == 0 else 128
    tiles = own // tile
    outs = width // wide
    inner_x = my_x + 1 - 2 * (my_x % 2)
    MESH = pl.DeviceIdType.MESH

    def host(offset, inner=False):
        z = lax.rem(my_z + offset[0], SIDE)
        x = my_x if offset[1] == 0 else SIDE - 1 - my_x
        if inner:
            x = x + 1 - 2 * (x % 2)
        return z * SIDE + x

    def device(offset):
        return (dp, host(offset))

    def toward(n):
        return device((0, 1)) if n == OUTER else device((STEP[n] % SIDE, 0))

    def back_from(n):
        return device((0, 1)) if n == OUTER else device((-STEP[n] % SIDE, 0))

    inner = (dp, my_z * SIDE + inner_x)
    cross = (dp + 1 - 2 * my_core, me)

    def plane(step):
        return lax.rem(my_y + step + SIDE, SIDE) * 2 + my_core

    def rows_of(c, offset, part):
        start = c * group + WHERE[offset] * rows
        if part is None:
            return start, rows
        return start + (0 if part == UP else rows // 2), rows // 2

    def region(c, cols, offset, part):
        start, size = rows_of(c, offset, part)
        return buf.at[pl.ds(start, size), pl.ds(*columns[cols])]

    def landing(c, copy):
        key, place = SPOT[copy]
        return landings[key].at[c, place]

    def gather_copy(c, copy):
        cols, q, part = block_of(*copy)
        n = copy[1]
        return pltpu.make_async_remote_copy(
            src_ref=region(c, cols, q, part), dst_ref=region(c, cols, moved(q, n), part),
            send_sem=ag_send.at[c, INDEX[copy]], recv_sem=ag_recv.at[c, INDEX[copy]],
            device_id=toward(n), device_id_type=MESH,
        )

    def reduce_copy(c, copy):
        cols, q, part = block_of(*copy)
        n = copy[1]
        return pltpu.make_async_remote_copy(
            src_ref=region(c, cols, moved(q, n), part), dst_ref=landing(c, copy),
            send_sem=rs_send.at[c, INDEX[copy]], recv_sem=rs_recv.at[c, INDEX[copy]],
            device_id=back_from(n), device_id_type=MESH,
        )

    def named(*kinds):
        return [copy for kind in kinds for copy in COPIES if copy[0] == kind]

    def start(make, c, *kinds):
        for copy in named(*kinds):
            make(c, copy).start()

    def arrive(make, c, *kinds):
        for copy in named(*kinds):
            make(c, copy).wait_recv()

    def sent(make, c):
        for copy in COPIES:
            make(c, copy).wait_send()

    def add(c, *kinds):
        where = {}
        for copy in named(*kinds):
            where.setdefault(block_of(*copy), []).append(landing(c, copy))
        for (cols, q, part), sources in where.items():
            base, size = rows_of(c, q, part)
            span = pl.ds(*columns[cols])

            @pl.loop(0, size // 16)
            def _(r):
                spot = pl.ds(pl.multiple_of(base + r * 16, 16), 16)
                total = buf[spot, span].astype(jnp.float32)
                for source in sources:
                    total += source[pl.ds(pl.multiple_of(r * 16, 16), 16), :].astype(jnp.float32)
                buf[spot, span] = total.astype(jnp.bfloat16)

    def ag(c, stage):
        if stage == 0:
            start(gather_copy, c, "Z1A", "Z1B", "O1A", "O1B")
        elif stage == 1:
            arrive(gather_copy, c, "O1A")
            start(gather_copy, c, "Z2")
        elif stage == 2:
            arrive(gather_copy, c, "Z1A", "Z1B")
            start(gather_copy, c, "O3", "O4", "Z3A", "Z3B")
        elif stage == 3:
            arrive(gather_copy, c, "Z2")
            start(gather_copy, c, "Z4")
        elif stage == 4:
            arrive(gather_copy, c, "Z3A", "Z3B")
            start(gather_copy, c, "O5")
        else:
            arrive(gather_copy, c, "O1B", "O3", "O4", "O5", "Z4")

    def rs(c, stage):
        if stage == 0:
            start(reduce_copy, c, "Z4", "Z3A", "O5", "O3", "O4", "O1B")
        elif stage == 1:
            arrive(reduce_copy, c, "Z4")
            add(c, "Z4")
            start(reduce_copy, c, "Z2")
        elif stage == 2:
            arrive(reduce_copy, c, "Z3A")
            add(c, "Z3A")
            start(reduce_copy, c, "Z1A")
        elif stage == 3:
            arrive(reduce_copy, c, "O5")
            add(c, "O5")
            start(reduce_copy, c, "Z3B")
        elif stage == 4:
            arrive(reduce_copy, c, "O3", "O4")
            add(c, "O3", "O4")
        elif stage == 5:
            arrive(reduce_copy, c, "Z3B")
            add(c, "Z3B")
            start(reduce_copy, c, "Z1B")
        elif stage == 6:
            arrive(reduce_copy, c, "Z2")
            add(c, "Z2")
            start(reduce_copy, c, "O1A")
        else:
            arrive(reduce_copy, c, "Z1A", "Z1B", "O1A", "O1B")
            add(c, "Z1A", "O1A", "Z1B", "O1B")
            result(c).start()

    def result(c):
        return pltpu.make_async_copy(
            buf.at[pl.ds(c * group, rows), :], out.at[pl.ds(c * rows, rows), :], osem.at[c]
        )

    def mine(c):
        return pltpu.make_async_copy(
            tokens.at[pl.ds(c * rows, rows), :], buf.at[pl.ds(c * group, rows), :], tsem.at[c]
        )

    def weights():
        copies = []
        for e in range(experts):
            span = pl.ds(e * ff, ff)
            copies.append(pltpu.make_async_copy(w_gate.at[e], wg.at[:, span], wsem.at[0, e]))
            copies.append(pltpu.make_async_copy(w_up.at[e], wu.at[:, span], wsem.at[1, e]))
            copies.append(pltpu.make_async_copy(w_down.at[e], wd.at[span, :], wsem.at[2, e]))
        return copies

    blocks = [(a, e) for a in range(3) for e in range(experts)]
    in_part, down_part = width // 8, ff // 8

    def slice_of(k, index):
        a, e = blocks[k]
        if a == 2:
            return wd.at[pl.ds(own + e * ff + index * down_part, down_part), :]
        return (wg, wu)[a].at[pl.ds(index * in_part, in_part), pl.ds(own + e * ff, ff)]

    def fetch(k):
        a, e = blocks[k]
        size = down_part if a == 2 else in_part
        return pltpu.make_async_remote_copy(
            src_ref=(w_gate, w_up, w_down)[a].at[e, pl.ds(dp * size, size), :], dst_ref=slice_of(k, dp),
            send_sem=x_send.at[k], recv_sem=x_recv.at[k], device_id=inner, device_id_type=MESH,
        )

    def spread(k, n):
        return pltpu.make_async_remote_copy(
            src_ref=slice_of(k, dp), dst_ref=slice_of(k, dp),
            send_sem=y_send.at[k, n], recv_sem=y_recv.at[k, n],
            device_id=(plane(STEP[n]), me), device_id_type=MESH,
        )

    def relay(k):
        n = UP if blocks[k][1] == 0 else DOWN
        source = plane(-STEP[n])
        return pltpu.make_async_remote_copy(
            src_ref=slice_of(k, source), dst_ref=slice_of(k, source),
            send_sem=r_send.at[k], recv_sem=r_recv.at[k],
            device_id=(plane(STEP[n]), me), device_id_type=MESH,
        )

    def across(k, m):
        source = plane((0, -1, 1, 2)[m])
        return pltpu.make_async_remote_copy(
            src_ref=slice_of(k, source), dst_ref=slice_of(k, source),
            send_sem=c_send.at[k, m], recv_sem=c_recv.at[k, m], device_id=cross, device_id_type=MESH,
        )

    def wx(k):
        fetch(k).wait_recv()
        spread(k, UP).start()
        spread(k, DOWN).start()
        across(k, 0).start()

    def wy(k):
        spread(k, UP).wait_recv()
        spread(k, DOWN).wait_recv()
        relay(k).start()
        across(k, 1).start()
        across(k, 2).start()

    def wr(k):
        relay(k).wait_recv()
        across(k, 3).start()

    def have(*ks):
        for k in ks:
            for m in range(4):
                across(k, m).wait_recv()

    def share_copy(offset):
        back = (-offset[0] % SIDE, offset[1])
        return pltpu.make_async_remote_copy(
            src_ref=sh_out.at[WHERE[offset]], dst_ref=sh_in.at[WHERE[back]],
            send_sem=sh_send.at[WHERE[offset]], recv_sem=sh_recv.at[WHERE[back]],
            device_id=device(offset), device_id_type=MESH,
        )

    def share_arrival(offset):
        return share_copy((-offset[0] % SIDE, offset[1]))

    lent_copy = pltpu.make_async_remote_copy(
        src_ref=lent, dst_ref=lent_in, send_sem=ln_send, recv_sem=ln_recv,
        device_id=inner, device_id_type=MESH,
    )

    for c in range(CHUNKS):
        mine(c).start()
    barrier = pltpu.get_barrier_semaphore()
    peers = [device(offset) for offset in ORDER[1:]]
    peers += [inner, cross, (plane(1), me), (plane(-1), me)]
    for peer in peers:
        pl.semaphore_signal(barrier, inc=1, device_id=peer, device_id_type=MESH)
    for c in range(CHUNKS):
        mine(c).wait()
    pl.semaphore_wait(barrier, len(peers))
    ag(0, 0)
    for k in range(len(blocks)):
        fetch(k).start()
    lent_copy.start()
    for copy in weights():
        copy.start()
    choice = target[...]
    share = weight[...]
    share = share / jnp.sum(share, axis=0, keepdims=True)
    slots = experts + 1
    count = SIDE * SIDE
    for offset in ORDER:
        row = 0
        for side in (False, True):
            place = host(offset, side)
            names = [place * slots + k for k in range(experts)]
            names.append(lax.rem(place + 1, count) * slots + experts)
            for slot in names:
                sh_out[WHERE[offset], row:row + 1, :] = jnp.sum(
                    jnp.where(choice == slot, share, 0.0), axis=0, keepdims=True
                )
                row += 1
        sh_out[WHERE[offset], row:8, :] = jnp.zeros((8 - row, share.shape[1]), jnp.float32)
    for offset in ORDER[1:]:
        share_copy(offset).start()
    sh_in[0] = sh_out[0]
    ag(0, 1)
    ag(0, 2)
    ag(0, 3)
    for offset in ORDER[1:]:
        share_arrival(offset).wait_recv()
    lent_copy.wait_recv()
    for p in range(len(ORDER)):
        for base, lend in ((0, lent), (3, lent_in)):
            second = lend[0:1, :]
            spare = sh_in[p, base + 2:base + 3, :]
            sh_in[p, base:base + 1, :] = sh_in[p, base:base + 1, :] + (1.0 - second) * spare
            sh_in[p, base + 1:base + 2, :] = sh_in[p, base + 1:base + 2, :] + second * spare
    both = 2 * rows
    for pair in range(CHUNKS // 2):
        table = jnp.concatenate([sh_in[p, :, pair * both:(pair + 1) * both] for p in range(len(ORDER))], axis=0)
        turned = jnp.transpose(table)
        for c in range(2):
            for p in range(len(ORDER)):
                base = (pair * 2 + c) * group + p * rows
                coef[base:base + rows, :] = turned[c * rows:(c + 1) * rows, p * 8:p * 8 + 8]
    wx(0)
    ag(0, 4)
    ag(1, 0)
    for copy in weights():
        copy.wait()
    ag(0, 5)

    def run(events, length, fn):
        @pl.loop(0, length)
        def _(i):
            for when in sorted(events):
                @pl.when(i == when)
                def _(calls=events[when]):
                    for call in calls:
                        call[0](*call[1:])
            fn(i)

    def hidden(first, second):
        def fn(i):
            g = first + i // tiles
            j = i % tiles
            cols = pl.ds(pl.multiple_of(j * tile + (own if second else 0), tile), tile)
            span = pl.ds(pl.multiple_of(g * group, group), group)
            x = buf[span, :]
            gate = jnp.dot(x, wg[:, cols], preferred_element_type=jnp.float32)
            upper = jnp.dot(x, wu[:, cols], preferred_element_type=jnp.float32)
            part = coef[span, :]
            lane = 3 if second else 0
            scale = jnp.where(j < tiles // experts, part[:, lane:lane + 1], part[:, lane + 1:lane + 2])
            value = gate / (1.0 + jnp.exp(-gate)) * upper * scale
            to = pl.ds(pl.multiple_of(j * tile, tile), tile)
            if second:
                hid_two[g % 2, :, to] = value.astype(jnp.bfloat16)
            else:
                hid[span, to] = value.astype(jnp.bfloat16)
        return fn

    def outward(first):
        def fn(i):
            g = first + i // outs
            cols = pl.ds(pl.multiple_of((i % outs) * wide, wide), wide)
            span = pl.ds(pl.multiple_of(g * group, group), group)
            y = jnp.dot(hid[span, :], wd[0:own, cols], preferred_element_type=jnp.float32)
            y += jnp.dot(hid_two[g % 2], wd[own:2 * own, cols], preferred_element_type=jnp.float32)
            buf[span, cols] = y.astype(jnp.bfloat16)
        return fn

    def events(*rows_):
        table = {}
        for g, j, fn, *args in rows_:
            table.setdefault(g * tiles + min(j, tiles - 1), []).append((fn, *args))
        return table

    def out_events(*rows_):
        table = {}
        for g, j, fn, *args in rows_:
            table.setdefault(g * outs + min(j, outs - 1), []).append((fn, *args))
        return table

    run(events(
        (0, 3, wx, 1), (0, 3, wy, 0), (0, 3, ag, 1, 1), (0, 3, ag, 1, 2), (0, 5, ag, 1, 3),
        (1, 0, ag, 1, 4), (1, 0, ag, 2, 0), (1, 0, wx, 2), (1, 0, wy, 1), (1, 0, ag, 1, 5),
        (1, 3, ag, 2, 1), (1, 3, ag, 2, 2), (1, 5, ag, 2, 3), (1, 5, wx, 3), (1, 5, wr, 0),
        (2, 0, ag, 2, 4), (2, 0, ag, 3, 0), (2, 0, wy, 2), (2, 0, ag, 2, 5),
        (2, 2, wx, 4), (2, 2, wr, 1), (2, 3, ag, 3, 1), (2, 3, ag, 3, 2), (2, 5, ag, 3, 3),
        (3, 0, ag, 3, 4), (3, 0, wx, 5), (3, 0, wy, 3), (3, 0, ag, 3, 5),
        (3, 5, wr, 2), (3, 5, wr, 3),
    ), CHUNKS * tiles, hidden(0, False))
    have(0, 1, 2, 3)
    run(events((0, 4, wy, 4), (1, 4, wy, 5)), 2 * tiles, hidden(0, True))
    wr(4)
    wr(5)
    have(4, 5)
    sent(gather_copy, 0)
    sent(gather_copy, 1)
    run(out_events(
        (1, 0, rs, 0, 0), (1, 1, rs, 0, 1), (1, 2, rs, 0, 2), (1, 2, rs, 0, 3),
    ), 2 * outs, outward(0))
    rs(0, 6)
    rs(0, 4)
    rs(1, 0)
    sent(gather_copy, 2)
    run(events((0, 2, rs, 0, 5), (0, 4, rs, 0, 7), (0, 5, rs, 1, 1)), tiles, hidden(2, True))
    run(out_events(
        (0, 0, rs, 1, 2), (0, 0, rs, 1, 3), (0, 2, rs, 1, 6), (0, 2, rs, 1, 4),
    ), outs, outward(2))
    rs(2, 0)
    sent(gather_copy, 3)
    run(events(
        (0, 0, rs, 1, 5), (0, 2, rs, 1, 7), (0, 3, rs, 2, 1), (0, 4, rs, 2, 2), (0, 4, rs, 2, 3),
    ), tiles, hidden(3, True))
    run(out_events(
        (0, 0, rs, 2, 6), (0, 0, rs, 2, 4), (0, 2, rs, 2, 5),
    ), outs, outward(3))
    rs(3, 0)
    rs(2, 7)
    for stage in (1, 2, 3, 6, 4, 5, 7):
        rs(3, stage)
    for c in range(CHUNKS):
        result(c).wait()
        sent(reduce_copy, c)
    for offset in ORDER[1:]:
        share_copy(offset).wait_send()
    lent_copy.wait_send()
    for k in range(len(blocks)):
        fetch(k).wait_send()
        spread(k, UP).wait_send()
        spread(k, DOWN).wait_send()
        relay(k).wait_send()
        for m in range(4):
            across(k, m).wait_send()


def body(tokens, target, router_weight, replica_pick, w_gate, w_up, w_down):
    tok_rows, width = tokens.shape
    experts, _, ff = w_gate.shape
    rows = tok_rows // CHUNKS
    places = len(ORDER)
    own = experts * ff
    split = width // 128 * 9 // 16 * 128
    wide = {"A": split, "B": width - split}
    lent = jnp.broadcast_to(replica_pick.astype(jnp.float32)[:, None], (8, tok_rows))
    any_space = pl.BlockSpec(memory_space=pl.ANY)
    vmem = pl.BlockSpec(memory_space=pltpu.VMEM)
    dma = pltpu.SemaphoreType.DMA
    landings = [
        pltpu.VMEM((CHUNKS, SIZES[key], rows // 2 if key[1] else rows, wide[key[0]]), jnp.bfloat16)
        for key in LANDINGS
    ]
    return pl.pallas_call(
        kernel,
        out_shape=jax.ShapeDtypeStruct((tok_rows, width), jnp.bfloat16),
        in_specs=[any_space, vmem, vmem, vmem, any_space, any_space, any_space],
        out_specs=any_space,
        scratch_shapes=[
            pltpu.VMEM((CHUNKS * places * rows, width), jnp.bfloat16),
            pltpu.VMEM((width, 2 * own), jnp.bfloat16),
            pltpu.VMEM((width, 2 * own), jnp.bfloat16),
            pltpu.VMEM((2 * own, width), jnp.bfloat16),
            pltpu.VMEM((places * tok_rows, own), jnp.bfloat16),
            pltpu.VMEM((2, places * rows, own), jnp.bfloat16),
            pltpu.VMEM((places * tok_rows, 8), jnp.float32),
            pltpu.VMEM((places, 8, tok_rows), jnp.float32),
            pltpu.VMEM((places, 8, tok_rows), jnp.float32),
            pltpu.VMEM((8, tok_rows), jnp.float32),
            *landings,
            dma((3, experts)),
            dma((CHUNKS,)),
            dma((CHUNKS,)),
            dma((CHUNKS, len(COPIES))),
            dma((CHUNKS, len(COPIES))),
            dma((CHUNKS, len(COPIES))),
            dma((CHUNKS, len(COPIES))),
            dma((places,)),
            dma((places,)),
            dma,
            dma,
            dma((3 * experts,)),
            dma((3 * experts,)),
            dma((3 * experts, 2)),
            dma((3 * experts, 2)),
            dma((3 * experts,)),
            dma((3 * experts,)),
            dma((3 * experts, 4)),
            dma((3 * experts, 4)),
        ],
        compiler_params=pltpu.CompilerParams(
            collective_id=0, has_side_effects=True, vmem_limit_bytes=67043328
        ),
        cost_estimate=pl.CostEstimate(
            flops=12 * places * tok_rows * width * ff * experts,
            bytes_accessed=6 * experts * width * ff * 2,
            transcendentals=2 * places * tok_rows * ff * experts,
        ),
        name="moe_layer",
    )(tokens, target.T, router_weight.T, lent, w_gate, w_up, w_down)


def solution(mesh):
    in_specs = (
        P(("dp", "expert"), None),
        P(("dp", "expert"), None),
        P(("dp", "expert"), None),
        P(("dp", "expert")),
        P("expert", None, None),
        P("expert", None, None),
        P("expert", None, None),
    )
    out_specs = P(("dp", "expert"), None)
    return jax.shard_map(body, mesh=mesh, in_specs=in_specs, out_specs=out_specs, check_vma=False)
```

time: 363 us -> 243 us (0.67)
  Pallas kernels: 0 us -> 239 us
  waiting for transfers between devices: 177 us -> 0 us
  matrix products: 121 us -> 0 us
  blocking collectives: 49.3 us -> 0 us
  between operations: 14.1 us -> 0.66 us
    pallas_call x0 -> x1, Pallas kernels: none -> 239 us  [body(): pl.pallas_call(kernel, out_shape=jax.ShapeDtypeStruct((tok_rows, width),...]
    dot_general x5 -> x0, matrix products: 121 us -> none  [the longest x2 47.6 us: body(): upper = jnp.dot(all_tokens, w_up[local], preferred_element_type=jnp.float32)]
    reduce_scatter x1 -> x0, waiting for transfers between devices: 111 us -> none  [body(): return lax.psum_scatter(partial, 'expert', scatter_dimension=0, tiled=True)]
    all_gather x1 -> x0, waiting for transfers between devices: 65.1 us -> none  [body(): all_tokens = lax.all_gather(tokens, 'expert', axis=0, tiled=True)]
    all_gather x2 -> x0, blocking collectives: 49.3 us -> none  [the longest x1 25.8 us: body(): all_share = lax.all_gather(share, 'expert', axis=0, tiled=True)]
  transfers between devices with their start and end apart: 2 -> 0, of which waited for: 2 -> 0; matrix products, arithmetic and copies ran while one was open for 0% -> 0% of each run, Pallas kernels for 0% -> 0%
where the time goes in v3:
time: 243 us
  Pallas kernels  239 us (98%)
  local copies, waits for them, and re-layouts  2.91 us (1%)
    pallas_call x1, Pallas kernels, body(): pl.pallas_call(kernel, out_shape=jax.ShapeDtypeStruct((tok_rows, width),...  239 us

profile of v3, /device:TPU:0, one launch (start us, length us, event | category | flops | bytes accessed | tf_op | source)
XLA Modules:
  0.0 242.6 jit_solution(14208228026715911410)
XLA Ops:
  0.7 0.6 broadcast_in_dim.9.lent
  1.3 239.1 %moe_layer.1 = bf16[256,2048]{1,0:T(8,128)(2,1)} custom-call(bf16[256,2048]{1,0:T(8,128)(2,1)} %tokens.1, s32[8,256]{1,0:T(8,128)} %bitcast.3, f32[8,256]{1,0:T(8,128)} %bitcast.4, f32[8,256]{1,0:T(8,128)} %broadcast_in_dim.9.lent, bf16[2,2048,768]{2,1,0:T(8,128)(2,1)} %w_gate.1, bf16[2,2048,768]{2,1,0:T(8,128)(2,1)} %w_up.1, bf16[2,768,2048]{2,1,0:T(8,128)(2,1)} %w_down.1), custom_call_target="tpu_custom_call" | custom-call | flops 77309411328 | bytes 37748736 | tf_op jit(solution)/shard_map/moe_layer/pallas_call | solution.py:489
  240.3 2.3 copy.10

commit v4 on v2

--- a/solution.py
+++ b/solution.py
@@ -138,12 +138,12 @@
             base = WHERE[q] * rows + part[0]
             cols = pl.ds(h * half, half)
 
-            @pl.loop(0, part[1] // 16)
+            @pl.loop(0, part[1] // 32)
             def _(r):
-                spot = pl.ds(pl.multiple_of(base + r * 16, 16), 16)
+                spot = pl.ds(pl.multiple_of(base + r * 32, 32), 32)
                 total = buf[b, spot, cols].astype(jnp.float32)
                 for source in sources:
-                    total += source[pl.ds(pl.multiple_of(r * 16, 16), 16), :].astype(jnp.float32)
+                    total += source[pl.ds(pl.multiple_of(r * 32, 32), 32), :].astype(jnp.float32)
                 buf[b, spot, cols] = total.astype(jnp.bfloat16)
 
     everywhere = range(4)
@@ -176,32 +176,34 @@
         elif stage == 8:
             arrive(gather_copy, c, (K8,))
 
+    def onward(c, kind, following):
+        for n in everywhere:
+            reduce_copy(c, kind, n).wait_recv()
+            add(c, [(kind, n)])
+            reduce_copy(c, following, n).start()
+
     def rs(c, stage):
         if stage == 0:
             start(reduce_copy, c, (K8, K6A, K6B, K5))
         elif stage == 1:
-            arrive(reduce_copy, c, (K8,))
-            add(c, each(K8))
-            start(reduce_copy, c, (K7,))
+            onward(c, K8, K7)
         elif stage == 2:
-            arrive(reduce_copy, c, (K6A, K6B))
-            add(c, each(K6A, K6B))
-            start(reduce_copy, c, (K4A, K4B))
+            onward(c, K6A, K4A)
+            onward(c, K6B, K4B)
         elif stage == 3:
-            arrive(reduce_copy, c, (K5,))
-            add(c, each(K5))
-            start(reduce_copy, c, (K2,))
+            onward(c, K5, K2)
         elif stage == 4:
-            arrive(reduce_copy, c, (K7,))
-            add(c, each(K7))
-            start(reduce_copy, c, (K3,))
+            for landed, freed in (((2, 3), (0, 1)), ((0, 1), (2, 3))):
+                for n in landed:
+                    reduce_copy(c, K7, n).wait_recv()
+                add(c, [(K7, n) for n in landed])
+                for n in freed:
+                    reduce_copy(c, K3, n).start()
         elif stage == 5:
             arrive(reduce_copy, c, (K4A, K4B))
             add(c, each(K4A, K4B))
         elif stage == 6:
-            arrive(reduce_copy, c, (K3,))
-            add(c, each(K3))
-            start(reduce_copy, c, (K1,))
+            onward(c, K3, K1)
         elif stage == 7:
             arrive(reduce_copy, c, (K2, K1))
             add(c, each(K2, K1))
@@ -247,6 +249,12 @@
         pl.semaphore_signal(
             barrier, inc=1, device_id=device(offset), device_id_type=pl.DeviceIdType.MESH
         )
+    for c in range(CHUNKS):
+        own(c).wait()
+    pl.semaphore_wait(barrier, len(ORDER) - 1)
+    ag(0, 0)
+    for copy in weights():
+        copy.start()
     choice = target[...]
     share = weight[...]
     share = share / jnp.sum(share, axis=0, keepdims=True)
@@ -261,12 +269,6 @@
             )
         for k in range(len(named), 8):
             sh_out[WHERE[offset], k:k + 1, :] = jnp.zeros((1, share.shape[1]), jnp.float32)
-    for c in range(CHUNKS):
-        own(c).wait()
-    pl.semaphore_wait(barrier, len(ORDER) - 1)
-    ag(0, 0)
-    for copy in weights():
-        copy.start()
     for offset in ORDER[1:]:
         share_copy(offset).start()
     sh_in[0] = sh_out[0]
@@ -306,13 +308,14 @@
     plan(4, 3, ag, 1, 4)
     plan(4, 6, sent, gather_copy, 0)
     plan(4, 6, ag, 1, 5)
-    plan(5, 1, ag, 1, 6)
-    plan(5, 1, rs, 0, 0)
-    plan(5, 5, ag, 1, 7)
+    plan(5, 0, ag, 1, 6)
+    plan(5, 0, rs, 0, 0)
+    plan(5, 0, ag, 1, 7)
     plan(5, 8, ag, 1, 8)
     plan(6, 1, rs, 0, 1)
     plan(6, 5, rs, 0, 2)
     plan(6, 8, rs, 0, 3)
+    plan(7, 0, rs, 1, 0)
     plan(7, 2, rs, 0, 4)
 
     @pl.loop(0, groups * steps)
@@ -325,7 +328,9 @@
         g = i // steps
         j = i % steps
         c = g // (groups // CHUNKS)
-        row0 = pl.multiple_of((g % (groups // CHUNKS)) * group_rows, group_rows)
+        turn = g % GROUP
+        place = (1 - c) * turn + c * ((turn + 2) // 3 * (turn % 3 + 1))
+        row0 = pl.multiple_of(place * group_rows, group_rows)
 
         @pl.when(j < hidden_tiles)
         def _():
@@ -333,7 +338,7 @@
             x = buf[c, pl.ds(row0, group_rows), :]
             gate = jnp.dot(x, wg[:, cols], preferred_element_type=jnp.float32)
             upper = jnp.dot(x, wu[:, cols], preferred_element_type=jnp.float32)
-            both = coef[pl.ds(pl.multiple_of(g * group_rows, group_rows), group_rows), :]
+            both = coef[pl.ds(pl.multiple_of((c * GROUP + place) * group_rows, group_rows), group_rows), :]
             scale = jnp.where(j < hidden_tiles // experts, both[:, 0:1], both[:, 1:2])
             value = gate / (1.0 + jnp.exp(-gate)) * upper * scale
             hid[:, cols] = value.astype(jnp.bfloat16)
@@ -344,7 +349,6 @@
             y = jnp.dot(hid[...], wd[:, cols], preferred_element_type=jnp.float32)
             buf[2 - 2 * c, pl.ds(row0, group_rows), cols] = y.astype(jnp.bfloat16)
 
-    rs(1, 0)
     rs(0, 5)
     rs(0, 6)
     rs(1, 1)

time: 198 us -> 197 us (level)
  no operation moved by 1% of the time
where the time goes in v4:
time: 197 us; the launch traced here: 196 us
  Pallas kernels  193 us (98%)
  local copies, waits for them, and re-layouts  2.9 us (1%)
    pallas_call x1, Pallas kernels, body(): pl.pallas_call(kernel, out_shape=jax.ShapeDtypeStruct((tok_rows, width),...  193 us

profile of v4, /device:TPU:0, one launch (start us, length us, event | category | flops | bytes accessed | tf_op | source)
XLA Modules:
  0.0 196.4 jit_solution(590066140035869754)
XLA Ops:
  0.7 0.6 broadcast_in_dim.9.lent
  1.2 192.9 %moe_layer.1 = bf16[256,2048]{1,0:T(8,128)(2,1)} custom-call(bf16[256,2048]{1,0:T(8,128)(2,1)} %tokens.1, s32[8,256]{1,0:T(8,128)} %bitcast.3, f32[8,256]{1,0:T(8,128)} %bitcast.4, f32[8,128]{1,0:T(8,128)} %broadcast_in_dim.9.lent, bf16[2,2048,768]{2,1,0:T(8,128)(2,1)} %w_gate.1, bf16[2,2048,768]{2,1,0:T(8,128)(2,1)} %w_up.1, bf16[2,768,2048]{2,1,0:T(8,128)(2,1)} %w_down.1), custom_call_target="tpu_custom_call" | custom-call | flops 77309411328 | bytes 18874368 | tf_op jit(solution)/shard_map/moe_layer/pallas_call | solution.py:381
  194.1 2.3 %copy.10 = bf16[256,2048]{1,0:T(8,128)(2,1)} copy(bf16[256,2048]{1,0:T(8,128)(2,1)} %moe_layer.1) | data formatting | bytes 2097152

commit v5 on v4

--- a/solution.py
+++ b/solution.py
@@ -349,9 +349,9 @@
             y = jnp.dot(hid[...], wd[:, cols], preferred_element_type=jnp.float32)
             buf[2 - 2 * c, pl.ds(row0, group_rows), cols] = y.astype(jnp.bfloat16)
 
+    rs(1, 1)
     rs(0, 5)
     rs(0, 6)
-    rs(1, 1)
     rs(1, 2)
     rs(1, 3)
     rs(0, 7)

time: 197 us -> 196 us (level)
  no operation moved by 1% of the time
where the time goes in v5:
time: 196 us
  Pallas kernels  193 us (98%)
  local copies, waits for them, and re-layouts  2.9 us (1%)
    pallas_call x1, Pallas kernels, body(): pl.pallas_call(kernel, out_shape=jax.ShapeDtypeStruct((tok_rows, width),...  193 us

profile of v5, /device:TPU:0, one launch (start us, length us, event | category | flops | bytes accessed | tf_op | source)
XLA Modules:
  0.0 196.3 jit_solution(14795654321379444375)
XLA Ops:
  0.7 0.6 broadcast_in_dim.9.lent
  1.2 192.7 %moe_layer.1 = bf16[256,2048]{1,0:T(8,128)(2,1)} custom-call(bf16[256,2048]{1,0:T(8,128)(2,1)} %tokens.1, s32[8,256]{1,0:T(8,128)} %bitcast.3, f32[8,256]{1,0:T(8,128)} %bitcast.4, f32[8,128]{1,0:T(8,128)} %broadcast_in_dim.9.lent, bf16[2,2048,768]{2,1,0:T(8,128)(2,1)} %w_gate.1, bf16[2,2048,768]{2,1,0:T(8,128)(2,1)} %w_up.1, bf16[2,768,2048]{2,1,0:T(8,128)(2,1)} %w_down.1), custom_call_target="tpu_custom_call" | custom-call | flops 77309411328 | bytes 18874368 | tf_op jit(solution)/shard_map/moe_layer/pallas_call | solution.py:381
  194.0 2.3 %copy.10 = bf16[256,2048]{1,0:T(8,128)(2,1)} copy(bf16[256,2048]{1,0:T(8,128)(2,1)} %moe_layer.1) | data formatting | bytes 2097152
